TPU v7x, 128 devices: a whole 4x4x4 slice. The times are simulated.
128 devices in a mesh: tile: 16 (over z_hi, x, core), frame: 8 (over y, z_lo).
Axes of the slice: x: 4, y: 4, z: 4 (z_hi: 2, z_lo: 2; z = z_hi * 2 + z_lo), core: 2. Of those that a mesh axis runs over, the one named last changes fastest.
Arguments:
- frames: bfloat16 [8, 512, 512], P('frame', 'tile'), may hold values from -6 to 6
- row_shifts: int32 [512, 8], P('frame'), may hold values from -16 to 16, as said below
- column_shifts: int32 [512, 8], P('frame'), may hold values from -16 to 16, as said below
- frame_inverse_weight: float32 [8], replicated, may hold values from 0.05 to 0.5
- psf_rows: float32 [13], replicated, may hold values from 0.1 to 0.4
- psf_cols: float32 [13], replicated, may hold values from 0.1 to 0.4
Outputs:
- filtered: bfloat16 [512, 512, 512], P('frame', 'tile')
Inputs may be any that keep to these rules, and one draw needn't show every extreme that they name: row_shifts[v, f] = floor(r_v * (2 f - 7) / 7) for an integer row rate r_v per velocity; both extremes are reached. column_shifts follows the same law with an integer column rate c_v per velocity; both extremes are reached; the rate pairs (r_v, c_v) are distinct across all 512 velocities.
All inputs are finite; a program needn't handle non-finite values.
Results may differ from a plain program's by a relative error of at most 0.005.
Values may be sent and summed in bfloat16 or wider, within the bound.
A program may use at most 64 MiB of HBM per device.

v0:
```python
import jax
import jax.numpy as jnp
from jax import lax
from jax.sharding import PartitionSpec as P

HALO = 16
RADIUS = 6


def extended_2(cells, sides, width):
    for axis, dim in sides:
        count = lax.axis_size(axis)
        ends = count - 1
        head = lax.slice_in_dim(cells, 0, width, axis=dim)
        tail = lax.slice_in_dim(cells, cells.shape[dim] - width, cells.shape[dim], axis=dim)
        cells = jnp.concatenate(
            [
                lax.ppermute(tail, axis, [(i, (i + 1) % count) for i in range(ends)]),
                cells,
                lax.ppermute(head, axis, [((i + 1) % count, i) for i in range(ends)]),
            ],
            axis=dim,
        )
    return cells


def shards(frames, row_shifts, column_shifts, frame_inverse_weight, psf_rows, psf_cols):
    rows = frames.shape[1]
    width = frames.shape[2]
    vel_count = row_shifts.shape[0]
    haloed = extended_2(frames, (("tile", 1),), HALO)
    stack_rows = haloed.shape[1] - 2 * HALO
    empty = jnp.zeros((vel_count, stack_rows, width), jnp.float32)
    piece = lax.all_gather(haloed, "frame", axis=0, tiled=True)

    def one_frame(index, acc):
        frame_image = jnp.pad(piece[index], ((0, 0), (HALO, HALO)))
        weight = lax.dynamic_index_in_dim(frame_inverse_weight, index, 0, keepdims=False)
        row_moves = lax.dynamic_index_in_dim(row_shifts, index, 1, keepdims=False)
        col_moves = lax.dynamic_index_in_dim(column_shifts, index, 1, keepdims=False)

        def window(row_move, col_move):
            return lax.dynamic_slice(
                frame_image, (HALO + row_move, HALO + col_move), (stack_rows, width)
            )

        moved = jax.vmap(window)(row_moves, col_moves)
        return acc + weight * moved.astype(jnp.float32)

    summed = lax.fori_loop(0, piece.shape[0], one_frame, empty)
    stacked = summed.astype(jnp.bfloat16)
    extended = extended_2(stacked, (("tile", 1),), RADIUS)
    rowpass = jnp.zeros((vel_count, rows, width), jnp.float32)
    for k in range(2 * RADIUS + 1):
        rowpass = rowpass + psf_rows[k] * extended[:, k : k + rows, :].astype(jnp.float32)
    wide_rows = jnp.pad(rowpass, ((0, 0), (0, 0), (RADIUS, RADIUS)))
    result = jnp.zeros((vel_count, rows, width), jnp.float32)
    for k in range(2 * RADIUS + 1):
        result = result + psf_cols[k] * wide_rows[:, :, k : k + width]
    return result.astype(jnp.bfloat16)


def solution(mesh):
    return jax.shard_map(
        shards,
        mesh=mesh,
        in_specs=(P("frame", "tile", None), P("frame", None), P("frame", None), P(), P(), P()),
        out_specs=P("frame", "tile", None),
        check_vma=False,
    )
```

profile of v0, /device:TPU:7, one launch (start us, length us, event | category | flops | bytes accessed | tf_op | source)
XLA Modules:
  0.0 1175.0 jit_solution(13267981951586405859)
XLA Ops:
  0.7 2.6 collective-permute-start.1
  3.3 6.6 collective-permute-start
  11.5 24.3 %all_gather.3 = bf16[8,64,512]{2,1,0:T(8,128)(2,1)S(1)} all-gather(bf16[1,64,512]{2,1,0:T(8,128)(2,1)S(1)} %pad_maximum_fusion.2), channel_id=1, replica_groups=mesh['tile'=16,'frame'=8] {'frame'}, dimensions={0}, use_global_device_ids=true | all-gather | bytes 589824 | tf_op jit(solution)/shard_map/all_gather | solution.py:34
  35.8 1075.9 %while.20 = (s32[]{:T(128)}, f32[64,32,512]{2,1,0:T(8,128)}, f32[8]{0:T(128)}, bf16[8,64,512]{2,1,0:T(8,128)(2,1)S(1)}, s32[64,8]{0,1:T(8,128)}, /*index=5*/s32[...) while((s32[]{:T(128)}, f32[64,32,512]{2,1,0:T(8,128)}, f32[8]{0:T(128)}, ...), condition=%wide.region_1.2_spmd.clone, body=%wide.region_0.1_spmd.clone.sunk | while | flops 4194949 | bytes 10819894 | solution.py:50
  36.6 126.7 %while.21 = (s32[]{:T(128)}, bf16[64,544]{1,0:T(8,128)(2,1)S(1)}, s32[64,2]{0,1:T(2,128)S(1)}, bf16[64,32,512]{2,1,0:T(8,128)(2,1)S(1)}, s32[]{:T(128)}) while((s32[]{:T(128)}, bf16[64,544]{1,0:T(8,128)(2,1)S(1)}, s32[64,2]{0,1:T(2,128)S(1)}, bf16[64,32,512]{2,1,0:T(8,128)(2,1)S(1)}, s32[]{:T(128)}) %tuple.88), condition=%wide.while_cond, body=%wide.while_body.sunk | while | flops 2 | bytes 65653 | solution.py:43
  37.3 1.3 bitcast_dynamic-update-slice_fusion.2
  39.3 1.3 bitcast_dynamic-update-slice_fusion.2
  41.3 1.3 bitcast_dynamic-update-slice_fusion.2
  43.2 1.3 bitcast_dynamic-update-slice_fusion.2
  45.2 1.3 bitcast_dynamic-update-slice_fusion.2
  47.2 1.3 bitcast_dynamic-update-slice_fusion.2
  164.7 3.7 select_add_fusion.2
  169.2 126.7 %while.21 = (s32[]{:T(128)}, bf16[64,544]{1,0:T(8,128)(2,1)S(1)}, s32[64,2]{0,1:T(2,128)S(1)}, bf16[64,32,512]{2,1,0:T(8,128)(2,1)S(1)}, s32[]{:T(128)}) while((s32[]{:T(128)}, bf16[64,544]{1,0:T(8,128)(2,1)S(1)}, s32[64,2]{0,1:T(2,128)S(1)}, bf16[64,32,512]{2,1,0:T(8,128)(2,1)S(1)}, s32[]{:T(128)}) %tuple.88), condition=%wide.while_cond, body=%wide.while_body.sunk | while | flops 2 | bytes 65653 | solution.py:43
  297.2 5.9 select_add_fusion.2
  304.0 126.7 %while.21 = (s32[]{:T(128)}, bf16[64,544]{1,0:T(8,128)(2,1)S(1)}, s32[64,2]{0,1:T(2,128)S(1)}, bf16[64,32,512]{2,1,0:T(8,128)(2,1)S(1)}, s32[]{:T(128)}) while((s32[]{:T(128)}, bf16[64,544]{1,0:T(8,128)(2,1)S(1)}, s32[64,2]{0,1:T(2,128)S(1)}, bf16[64,32,512]{2,1,0:T(8,128)(2,1)S(1)}, s32[]{:T(128)}) %tuple.88), condition=%wide.while_cond, body=%wide.while_body.sunk | while | flops 2 | bytes 65653 | solution.py:43
  432.0 5.9 select_add_fusion.2
  438.7 126.7 %while.21 = (s32[]{:T(128)}, bf16[64,544]{1,0:T(8,128)(2,1)S(1)}, s32[64,2]{0,1:T(2,128)S(1)}, bf16[64,32,512]{2,1,0:T(8,128)(2,1)S(1)}, s32[]{:T(128)}) while((s32[]{:T(128)}, bf16[64,544]{1,0:T(8,128)(2,1)S(1)}, s32[64,2]{0,1:T(2,128)S(1)}, bf16[64,32,512]{2,1,0:T(8,128)(2,1)S(1)}, s32[]{:T(128)}) %tuple.88), condition=%wide.while_cond, body=%wide.while_body.sunk | while | flops 2 | bytes 65653 | solution.py:43
  566.8 5.9 select_add_fusion.2
  573.5 126.7 %while.21 = (s32[]{:T(128)}, bf16[64,544]{1,0:T(8,128)(2,1)S(1)}, s32[64,2]{0,1:T(2,128)S(1)}, bf16[64,32,512]{2,1,0:T(8,128)(2,1)S(1)}, s32[]{:T(128)}) while((s32[]{:T(128)}, bf16[64,544]{1,0:T(8,128)(2,1)S(1)}, s32[64,2]{0,1:T(2,128)S(1)}, bf16[64,32,512]{2,1,0:T(8,128)(2,1)S(1)}, s32[]{:T(128)}) %tuple.88), condition=%wide.while_cond, body=%wide.while_body.sunk | while | flops 2 | bytes 65653 | solution.py:43
  701.5 5.9 select_add_fusion.2
  708.2 126.7 %while.21 = (s32[]{:T(128)}, bf16[64,544]{1,0:T(8,128)(2,1)S(1)}, s32[64,2]{0,1:T(2,128)S(1)}, bf16[64,32,512]{2,1,0:T(8,128)(2,1)S(1)}, s32[]{:T(128)}) while((s32[]{:T(128)}, bf16[64,544]{1,0:T(8,128)(2,1)S(1)}, s32[64,2]{0,1:T(2,128)S(1)}, bf16[64,32,512]{2,1,0:T(8,128)(2,1)S(1)}, s32[]{:T(128)}) %tuple.88), condition=%wide.while_cond, body=%wide.while_body.sunk | while | flops 2 | bytes 65653 | solution.py:43
  836.3 5.9 select_add_fusion.2
  843.0 126.7 %while.21 = (s32[]{:T(128)}, bf16[64,544]{1,0:T(8,128)(2,1)S(1)}, s32[64,2]{0,1:T(2,128)S(1)}, bf16[64,32,512]{2,1,0:T(8,128)(2,1)S(1)}, s32[]{:T(128)}) while((s32[]{:T(128)}, bf16[64,544]{1,0:T(8,128)(2,1)S(1)}, s32[64,2]{0,1:T(2,128)S(1)}, bf16[64,32,512]{2,1,0:T(8,128)(2,1)S(1)}, s32[]{:T(128)}) %tuple.88), condition=%wide.while_cond, body=%wide.while_body.sunk | while | flops 2 | bytes 65653 | solution.py:43
  971.0 5.9 select_add_fusion.2
  977.7 126.7 %while.21 = (s32[]{:T(128)}, bf16[64,544]{1,0:T(8,128)(2,1)S(1)}, s32[64,2]{0,1:T(2,128)S(1)}, bf16[64,32,512]{2,1,0:T(8,128)(2,1)S(1)}, s32[]{:T(128)}) while((s32[]{:T(128)}, bf16[64,544]{1,0:T(8,128)(2,1)S(1)}, s32[64,2]{0,1:T(2,128)S(1)}, bf16[64,32,512]{2,1,0:T(8,128)(2,1)S(1)}, s32[]{:T(128)}) %tuple.88), condition=%wide.while_cond, body=%wide.while_body.sunk | while | flops 2 | bytes 65653 | solution.py:43
  1105.8 5.9 select_add_fusion.2
  1111.7 2.5 convert_element_type.65
  1114.3 5.1 collective-permute-start.3
  1119.5 10.0 collective-permute-start.2
  1130.9 3.5 collective-permute-done.3
  1135.6 17.1 %multiply_add_fusion = f32[64,32,512]{2,1,0:T(8,128)S(1)} fusion(bf16[64,32,512]{2,1,0:T(8,128)(2,1)S(1)} %convert_element_type.65, bf16[64,6,512]{2,1,0:T(8,128)(2,1)S(1)} %collective-permute-done.3, bf16[64,6,512]{2,1,0:T(8,128)(2,1)S(1)} %collective-permute-done.2, f32[]{:T(128)} %bitcast.13, f32[]{:T(128)} %bitcast.12, f32[]{:T(128)} %bitcast.11, ...), kind=kLoop, calls=%fused_computation.55 | loop fusion | flops 77594624 | bytes 7077940 | tf_op jit(solution)/shard_map/add | solution.py:55
  1152.7 22.3 %fusion.24 = bf16[64,32,512]{2,1,0:T(8,128)(2,1)} fusion(f32[64,32,512]{2,1,0:T(8,128)S(1)} %multiply_add_fusion, f32[]{:T(128)} %bitcast.25, f32[]{:T(128)} %bitcast.24, f32[]{:T(128)} %bitcast.23, f32[]{:T(128)} %bitcast.22, f32[]{:T(128)} %bitcast.21, f32[]{:T(128)} %bitcast.20, f32[]{:T(128)} %bitcast.19, f32[]{:T(128)} %bitcast.18, f32[]{:T(128)} %bitcast.17, ...), kind=kLoop, calls=%fused_computation.56 | loop fusion | flops 27262976 | bytes 6291508 | tf_op jit(solution)/shard_map/convert_element_type | solution.py:60
  (1591 shorter events, 1027.2 us)
Async XLA Ops:
  0.7 9.2 collective-permute-start.1
  3.3 7.4 collective-permute-start
  1111.7 17.9 %copy-start = (f32[13]{0:T(128)S(1)}, f32[13]{0:T(128)}, u32[]{:S(2)}) copy-start(f32[13]{0:T(128)} %param.12) | copy-start | bytes 160
  1111.7 18.6 %copy-start.1 = (f32[13]{0:T(128)S(1)}, f32[13]{0:T(128)}, u32[]{:S(2)}) copy-start(f32[13]{0:T(128)} %param.13) | copy-start | bytes 160
  1114.3 20.1 %collective-permute-start.3 = (bf16[64,6,512]{2,1,0:T(8,128)(2,1)S(1)}, bf16[64,6,512]{2,1,0:T(8,128)(2,1)S(1)}, u32[]{:S(2)}, u32[]{:S(2)}) collective-permute-start(bf16[64,6,512]{2,1,0:T(8,128)(2,1)S(1)} %get-tuple-element.217), channel_id=1, source_target_pairs={{8,0},{16,8},{24,16},{32,24},{40,32},{48,40},{56,48},{64,56},{72,6... | collective-permute-start | bytes 1179656 | tf_op jit(solution)/shard_map/ppermute | solution.py:20
  1119.5 16.1 %collective-permute-start.2 = (bf16[64,6,512]{2,1,0:T(8,128)(2,1)S(1)}, bf16[64,6,512]{2,1,0:T(8,128)(2,1)S(1)}, u32[]{:S(2)}, u32[]{:S(2)}) collective-permute-start(bf16[64,6,512]{2,1,0:T(8,128)(2,1)S(1)} %get-tuple-element.216), channel_id=1, source_target_pairs={{0,8},{8,16},{16,24},{24,32},{32,40},{40,48},{48,56},{56,64},{64,7... | collective-permute-start | bytes 1179656 | tf_op jit(solution)/shard_map/ppermute | solution.py:18
where the time goes:
time: 1190 us; the launch traced here: 1180 us
  local copies, waits for them, and re-layouts  1030 us (87%)
  other arithmetic  93.3 us (8%)
  starting transfers between devices  24.3 us (2%)
  blocking collectives  24.3 us (2%)
    gather x1536, local copies, waits for them, and re-layouts  1010 us
    add x8, other arithmetic, one_frame(): return acc + weight * moved.astype(jnp.float32)  44.8 us
    all_gather x1, blocking collectives, shards(): piece = lax.all_gather(haloed, 'frame', axis=0, tiled=True)  24.3 us
  transfers between devices with their start and end apart: 4, of which 3 were waited for; matrix products, arithmetic and copies ran while one was open for 0% of the time, Pallas kernels for 0%

commit v1 on v0

v1 whole, which is shorter than its diff:
```python
import functools

import jax
import jax.numpy as jnp
from jax import lax
from jax.experimental import pallas as pl
from jax.experimental.pallas import tpu as pltpu
from jax.sharding import PartitionSpec as P

MESH = pl.DeviceIdType.MESH
HALO = 16
RADIUS = 6
TAPS = 2 * RADIUS + 1
FRAMES = 8
LANES = 128
STEP = 4
EDGE = 24
BAND = 32
TALL = BAND + 2 * EDGE
CUT = 40


def spans():
    out = []
    row = cut = 0
    for f in range(FRAMES):
        ends = [r * (2 * f - (FRAMES - 1)) // (FRAMES - 1) for r in (-HALO, HALO)]
        low, high = min(ends), max(ends)
        top = -(-(-low) // 8) * 8
        below = -(-high // 8) * 8
        count = high - low + STEP
        tall = top + BAND + below
        out.append((low, count, top, tall, row, cut))
        row += count * tall
        cut += count * CUT
    return out, row, cut


SPANS, TABLE_ROWS, CUT_ROWS = spans()


def gather_kernel(tiles, band_ref, all_ref, send, got, top_send, top_got, low_send, low_got):
    tile = lax.axis_index("tile")
    frame = lax.axis_index("frame")
    above, below = tile > 0, tile < tiles - 1
    peers = [lax.rem(frame + d, FRAMES) for d in range(1, FRAMES)]

    barrier = pltpu.get_barrier_semaphore()
    for peer in peers:
        pl.semaphore_signal(barrier, inc=1, device_id={"frame": peer}, device_id_type=MESH)

    @pl.when(above)
    def _():
        pl.semaphore_signal(barrier, inc=1, device_id={"tile": tile - 1}, device_id_type=MESH)

    @pl.when(below)
    def _():
        pl.semaphore_signal(barrier, inc=1, device_id={"tile": tile + 1}, device_id_type=MESH)

    pl.semaphore_wait(barrier, FRAMES - 1 + jnp.minimum(tile, 1) + jnp.minimum(tiles - 1 - tile, 1))

    def band_copy(peer, slot, source):
        return pltpu.make_async_remote_copy(
            src_ref=band_ref.at[0],
            dst_ref=all_ref.at[source, pl.ds(EDGE, BAND)],
            send_sem=send.at[slot],
            recv_sem=got.at[slot],
            device_id={"frame": peer},
            device_id_type=MESH,
        )

    def edge_copies(ref, slot, source):
        up = pltpu.make_async_remote_copy(
            src_ref=ref.at[pl.ds(0, EDGE)],
            dst_ref=all_ref.at[source, pl.ds(EDGE + BAND, EDGE)],
            send_sem=low_send.at[slot],
            recv_sem=low_got.at[slot],
            device_id={"tile": jnp.maximum(tile - 1, 0)},
            device_id_type=MESH,
        )
        down = pltpu.make_async_remote_copy(
            src_ref=ref.at[pl.ds(BAND - EDGE, EDGE)],
            dst_ref=all_ref.at[source, pl.ds(0, EDGE)],
            send_sem=top_send.at[slot],
            recv_sem=top_got.at[slot],
            device_id={"tile": jnp.minimum(tile + 1, tiles - 1)},
            device_id_type=MESH,
        )
        return up, down

    def forward(ref, slot, source):
        up, down = edge_copies(ref, slot, source)

        @pl.when(above)
        def _():
            up.start()

        @pl.when(below)
        def _():
            down.start()

    for d in range(1, FRAMES):
        band_copy(peers[d - 1], d, frame).start()
    forward(band_ref.at[0], 0, frame)
    all_ref[frame, pl.ds(EDGE, BAND)] = band_ref[0]

    @pl.when(jnp.logical_not(above))
    def _():
        all_ref[:, pl.ds(0, EDGE)] = jnp.zeros((FRAMES, EDGE, all_ref.shape[2]), all_ref.dtype)

    @pl.when(jnp.logical_not(below))
    def _():
        all_ref[:, pl.ds(EDGE + BAND, EDGE)] = jnp.zeros((FRAMES, EDGE, all_ref.shape[2]), all_ref.dtype)

    for d in range(1, FRAMES):
        source = lax.rem(frame + FRAMES - d, FRAMES)
        band_copy(peers[d - 1], d, source).wait_recv()
        forward(all_ref.at[source, pl.ds(EDGE, BAND)], d, source)
    for d in range(FRAMES):
        source = lax.rem(frame + FRAMES - d, FRAMES)
        up, down = edge_copies(all_ref.at[source, pl.ds(EDGE, BAND)], d, source)

        @pl.when(above)
        def _():
            up.wait_send()
            down.wait_recv()

        @pl.when(below)
        def _():
            down.wait_send()
            up.wait_recv()

    for d in range(1, FRAMES):
        band_copy(peers[d - 1], d, frame).wait_send()


def gather(tiles, frames):
    width = frames.shape[2]
    pair = pltpu.SemaphoreType.DMA((FRAMES,))
    return pl.pallas_call(
        functools.partial(gather_kernel, tiles),
        out_shape=jax.ShapeDtypeStruct((FRAMES, TALL, width), frames.dtype),
        in_specs=[pl.BlockSpec(memory_space=pltpu.VMEM)],
        out_specs=pl.BlockSpec(memory_space=pltpu.VMEM),
        scratch_shapes=[pair] * 6,
        compiler_params=pltpu.CompilerParams(collective_id=0, has_side_effects=True),
        name="gather",
    )(frames)


def stack_kernel(
    tile_of, tiles, group,
    row_ref, col_ref, weight_ref, psf_row_ref, psf_col_ref, all_ref, out_ref,
    table, cuts, order, banded, plain, coefs, sums,
):
    width = all_ref.shape[2]
    tile = tile_of()
    first, last = tile == 0, tile == tiles - 1
    edge = jnp.logical_or(first, last)

    @pl.when(pl.program_id(0) == 0)
    def _():
        x = lax.broadcasted_iota(jnp.int32, (width, LANES), 0)
        lane = lax.broadcasted_iota(jnp.int32, (width, LANES), 1)
        for j in range(STEP):
            order[:, j * LANES:(j + 1) * LANES] = jnp.where(x == STEP * lane + j, 1.0, 0.0).astype(jnp.bfloat16)

        banded[...] = jnp.zeros_like(banded)
        for j in range(STEP):
            for n in range(width // LANES):
                low = max(0, 32 * n - 16)
                high = min(LANES, 32 * n + 48)
                where = (
                    STEP * (lax.broadcasted_iota(jnp.int32, (high - low, LANES), 0) + low) + j
                    - lax.broadcasted_iota(jnp.int32, (high - low, LANES), 1) - n * LANES + RADIUS
                )
                block = jnp.zeros((high - low, LANES), jnp.float32)
                for k in range(TAPS):
                    block = jnp.where(where == k, psf_col_ref[k], block)
                banded[j * LANES + low:j * LANES + high, n * LANES:(n + 1) * LANES] = block.astype(jnp.bfloat16)

        s = lax.broadcasted_iota(jnp.int32, (8, LANES), 0)
        for u in range(RADIUS):
            top = jnp.zeros((8, LANES), jnp.float32)
            low = jnp.zeros((8, LANES), jnp.float32)
            for k in range(RADIUS):
                top = jnp.where(u - s == k, psf_row_ref[k], top)
                low = jnp.where(14 + u - s == k + RADIUS + 1, psf_row_ref[k + RADIUS + 1], low)
            coefs[u * 8:u * 8 + 8, :] = jnp.where(first, top, low)

        lanes = lax.broadcasted_iota(jnp.int32, (8, LANES), 1)

        def turned(value, q):
            if q == 0:
                return value
            moved = pltpu.roll(value, (-q) % LANES, 1)
            keep = lanes < LANES - q if q > 0 else lanes >= -q
            return jnp.where(jnp.broadcast_to(keep[:1], moved.shape), moved, 0.0)

        for f, (low, count, top, tall, row, cut) in enumerate(SPANS):
            picked = jnp.dot(all_ref[f], order[...], preferred_element_type=jnp.float32)
            for j in range(STEP):
                plain[j * TALL:(j + 1) * TALL, :] = picked[:, j * LANES:(j + 1) * LANES]
            taps = [psf_row_ref[k] * weight_ref[f] for k in range(TAPS)]
            for j in range(STEP):
                start = j * TALL + EDGE - top - RADIUS
                total = taps[0] * plain[start:start + tall, :]
                for k in range(1, TAPS):
                    total = total + taps[k] * plain[start + k:start + k + tall, :]
                for n in range(count):
                    if (low + n - j) % STEP == 0:
                        table[row + n * tall:row + (n + 1) * tall, :] = turned(total, (low + n - j) // STEP)

            @pl.when(edge)
            def _():
                for j in range(STEP):
                    start = j * TALL + jnp.where(first, EDGE - RADIUS - HALO, EDGE + BAND - HALO)
                    value = weight_ref[f] * plain[pl.ds(start, CUT), :]
                    for n in range(count):
                        if (low + n - j) % STEP == 0:
                            cuts[cut + n * CUT:cut + (n + 1) * CUT, :] = turned(value, (low + n - j) // STEP)

    def velocity(v, at_edge):
        vel = pl.program_id(0) * group + v
        rows, cut_rows = [], []
        for f, (low, count, top, tall, row, cut) in enumerate(SPANS):
            r = row_ref[f, vel]
            c = col_ref[f, vel] - low
            rows.append(c * tall + (r + (top + row)))
            cut_rows.append(c * CUT + (r + (HALO + cut)))
        for j in range(STEP):
            total = None
            for f, span in enumerate(SPANS):
                piece = table[pl.ds(rows[f] + j * span[3], BAND), :]
                total = piece if total is None else total + piece
            if at_edge:
                outside = None
                for f in range(FRAMES):
                    piece = cuts[pl.ds(cut_rows[f] + j * CUT, 8), :]
                    outside = piece if outside is None else outside + piece
                fix = None
                for u in range(RADIUS):
                    term = coefs[u * 8:u * 8 + 8, :] * jnp.broadcast_to(outside[u:u + 1], (8, LANES))
                    fix = term if fix is None else fix + term
                total = jnp.concatenate(
                    [
                        total[:8] - jnp.where(first, fix, 0.0),
                        total[8:24],
                        total[24:] - jnp.where(last, fix, 0.0),
                    ],
                    axis=0,
                )
            sums[pl.ds(pl.multiple_of(v * BAND, BAND), BAND), j * LANES:(j + 1) * LANES] = total.astype(jnp.bfloat16)

    @pl.when(edge)
    def _():
        @pl.loop(0, group)
        def _(v):
            velocity(v, True)

    @pl.when(jnp.logical_not(edge))
    def _():
        @pl.loop(0, group)
        def _(v):
            velocity(v, False)

    result = jnp.dot(sums[...], banded[...], preferred_element_type=jnp.float32)
    out_ref[...] = result.astype(out_ref.dtype).reshape(out_ref.shape)


def stacked(tile_of, tiles, everything, row_shifts, column_shifts, weights, psf_rows, psf_cols, group=16):
    vels = row_shifts.shape[0]
    width = everything.shape[2]
    smem = pl.BlockSpec(memory_space=pltpu.SMEM)
    return pl.pallas_call(
        functools.partial(stack_kernel, tile_of, tiles, group),
        out_shape=jax.ShapeDtypeStruct((vels, BAND, width), jnp.bfloat16),
        grid=(vels // group,),
        in_specs=[smem] * 5 + [pl.BlockSpec((FRAMES, TALL, width), lambda i: (0, 0, 0))],
        out_specs=pl.BlockSpec((group, BAND, width), lambda i: (i, 0, 0)),
        scratch_shapes=[
            pltpu.VMEM((TABLE_ROWS, LANES), jnp.float32),
            pltpu.VMEM((CUT_ROWS, LANES), jnp.float32),
            pltpu.VMEM((width, width), jnp.bfloat16),
            pltpu.VMEM((width, width), jnp.bfloat16),
            pltpu.VMEM((STEP * TALL, LANES), jnp.float32),
            pltpu.VMEM((RADIUS * 8, LANES), jnp.float32),
            pltpu.VMEM((group * BAND, width), jnp.bfloat16),
        ],
        compiler_params=pltpu.CompilerParams(vmem_limit_bytes=48 << 20),
        name="stack",
    )(row_shifts.T, column_shifts.T, weights, psf_rows, psf_cols, everything)


def shards(tiles, frames, row_shifts, column_shifts, frame_inverse_weight, psf_rows, psf_cols):
    everything = gather(tiles, frames)
    return stacked(
        lambda: lax.axis_index("tile"), tiles, everything,
        row_shifts, column_shifts, frame_inverse_weight, psf_rows, psf_cols,
    )


def solution(mesh):
    return jax.shard_map(
        functools.partial(shards, mesh.shape["tile"]),
        mesh=mesh,
        in_specs=(P("frame", "tile", None), P("frame", None), P("frame", None), P(), P(), P()),
        out_specs=P("frame", "tile", None),
        check_vma=False,
    )
```

time: 1190 us -> 34 us (0.03); the launches traced: 1180 us -> 33.7 us
  local copies, waits for them, and re-layouts: 1030 us -> 4.42 us
  other arithmetic: 93.3 us -> 0 us
  Pallas kernels: 0 us -> 29.2 us
  blocking collectives: 24.3 us -> 0 us
  starting transfers between devices: 24.3 us -> 0 us
    gather x1536 -> x0, local copies, waits for them, and re-layouts: 1010 us -> none
    add x9 -> x0, other arithmetic: 61.9 us -> none  [the longest x8 44.8 us: one_frame(): return acc + weight * moved.astype(jnp.float32)]
    pallas_call x0 -> x2, Pallas kernels: none -> 29.2 us  [the longest x1 17.8 us: gather(): pl.pallas_call(functools.partial(gather_kernel, tiles), out_shape=jax.Sha...]
    convert_element_type x2 -> x0, other arithmetic: 24.8 us -> none  [the longest x1 22.3 us: shards(): return result.astype(jnp.bfloat16)]
    ppermute x4 -> x0, starting transfers between devices: 24.3 us -> none  [the longest x2 16.6 us: extended_2(): lax.ppermute(tail, axis, [(i, (i + 1) % count) for i in range(ends)])]
    all_gather x1 -> x0, blocking collectives: 24.3 us -> none  [shards(): piece = lax.all_gather(haloed, 'frame', axis=0, tiled=True)]
  transfers between devices with their start and end apart: 4 -> 0, of which waited for: 3 -> 0; matrix products, arithmetic and copies ran while one was open for 0% -> 0% of each run, Pallas kernels for 0% -> 0%
where the time goes in v1:
time: 34 us; the launch traced here: 33.7 us
  Pallas kernels  29.2 us (86%)
  local copies, waits for them, and re-layouts  4.42 us (13%)
    pallas_call x1, Pallas kernels, gather(): pl.pallas_call(functools.partial(gather_kernel, tiles), out_shape=jax.Sha...  17.8 us
    pallas_call x1, Pallas kernels, stacked(): pl.pallas_call(functools.partial(stack_kernel, tile_of, tiles, group), ou...  11.4 us
    unnamed x12, local copies, waits for them, and re-layouts  4.42 us

profile of v1, /device:TPU:7, one launch (start us, length us, event | category | flops | bytes accessed | tf_op | source)
XLA Modules:
  0.0 33.7 jit_solution(11667504348820371806)
XLA Ops:
  0.0 17.8 %gather.1.all_ref = bf16[8,80,512]{2,1,0:T(8,128)(2,1)} custom-call(bf16[1,32,512]{2,1,0:T(8,128)(2,1)} %band_ref.1), custom_call_target="tpu_custom_call" | custom-call | tf_op jit(solution)/shard_map/gather/pallas_call | solution.py:140
  17.8 0.0 copy-start
  17.9 1.1 %copy-done = bf16[8,80,512]{2,1,0:T(8,128)(2,1)S(1)} copy-done((bf16[8,80,512]{2,1,0:T(8,128)(2,1)S(1)}, bf16[8,80,512]{2,1,0:T(8,128)(2,1)}, u32[]{:S(2)}) %copy-start) | copy-done | bytes 655384
  18.9 0.0 copy-start.1
  18.9 0.7 %copy-done.1 = s32[64,8]{0,1:T(8,128)S(1)} copy-done((s32[64,8]{0,1:T(8,128)S(1)}, s32[64,8]{0,1:T(8,128)}, u32[]{:S(2)}) %copy-start.1) | copy-done | bytes 2072
  19.6 0.0 copy-start.2
  19.6 0.7 %copy-done.2 = s32[64,8]{0,1:T(8,128)S(1)} copy-done((s32[64,8]{0,1:T(8,128)S(1)}, s32[64,8]{0,1:T(8,128)}, u32[]{:S(2)}) %copy-start.2) | copy-done | bytes 2072
  20.3 0.0 copy-start.3
  20.3 0.7 %copy-done.3 = f32[8]{0:T(128)S(1)} copy-done((f32[8]{0:T(128)S(1)}, f32[8]{0:T(128)}, u32[]{:S(2)}) %copy-start.3) | copy-done | bytes 56
  21.0 0.0 copy-start.4
  21.0 0.7 %copy-done.4 = f32[13]{0:T(128)S(1)} copy-done((f32[13]{0:T(128)S(1)}, f32[13]{0:T(128)}, u32[]{:S(2)}) %copy-start.4) | copy-done | bytes 76
  21.6 0.0 copy-start.5
  21.6 0.7 %copy-done.5 = f32[13]{0:T(128)S(1)} copy-done((f32[13]{0:T(128)S(1)}, f32[13]{0:T(128)}, u32[]{:S(2)}) %copy-start.5) | copy-done | bytes 76
  22.3 11.4 %stack.1 = bf16[64,32,512]{2,1,0:T(8,128)(2,1)} custom-call(s32[8,64]{1,0:T(8,128)S(1)} %bitcast.2, s32[8,64]{1,0:T(8,128)S(1)} %bitcast.3, f32[8]{0:T(128)S(1)} %copy-done.3, f32[13]{0:T(128)S(1)} %copy-done.4, f32[13]{0:T(128)S(1)} %copy-done.5, bf16[8,80,512]{2,1,0:T(8,128)(2,1)S(1)} %copy-done), custom_call_target="tpu_custom_call" | custom-call | tf_op jit(solution)/shard_map/stack/pallas_call | solution.py:275
Async XLA Ops:
  17.8 1.1 %copy-start = (bf16[8,80,512]{2,1,0:T(8,128)(2,1)S(1)}, bf16[8,80,512]{2,1,0:T(8,128)(2,1)}, u32[]{:S(2)}) copy-start(bf16[8,80,512]{2,1,0:T(8,128)(2,1)} %gather.1.all_ref) | copy-start | bytes 1966084
  18.9 0.7 %copy-start.1 = (s32[64,8]{0,1:T(8,128)S(1)}, s32[64,8]{0,1:T(8,128)}, u32[]{:S(2)}) copy-start(s32[64,8]{0,1:T(8,128)} %param.7) | copy-start | bytes 6148
  19.6 0.7 %copy-start.2 = (s32[64,8]{0,1:T(8,128)S(1)}, s32[64,8]{0,1:T(8,128)}, u32[]{:S(2)}) copy-start(s32[64,8]{0,1:T(8,128)} %param.8) | copy-start | bytes 6148
  20.3 0.7 %copy-start.3 = (f32[8]{0:T(128)S(1)}, f32[8]{0:T(128)}, u32[]{:S(2)}) copy-start(f32[8]{0:T(128)} %weight_ref.1) | copy-start | bytes 100
  21.0 0.7 %copy-start.4 = (f32[13]{0:T(128)S(1)}, f32[13]{0:T(128)}, u32[]{:S(2)}) copy-start(f32[13]{0:T(128)} %psf_row_ref.1) | copy-start | bytes 160
  21.6 0.7 %copy-start.5 = (f32[13]{0:T(128)S(1)}, f32[13]{0:T(128)}, u32[]{:S(2)}) copy-start(f32[13]{0:T(128)} %psf_col_ref.1) | copy-start | bytes 160
